TPU v7x, 32 devices: a whole 2x2x4 slice. The times are simulated.
32 devices in a mesh: sub: 4 (over z), grp: 8 (over y, x, core).
Axes of the slice: x: 2, y: 2, z: 4, core: 2. Of those that a mesh axis runs over, the one named last changes fastest.
Arguments:
- schur: bfloat16 [128, 1024, 1024], P(('sub', 'grp')), as said below
- mortar: bfloat16 [128, 8, 128, 128], P(('sub', 'grp')), may hold values from -0.5 to 0.5
- partner: int32 [128, 4], P(('sub', 'grp')), may hold values from 0 to 15, as said below
- corner_map: int32 [128, 8], P(('sub', 'grp')), may hold values from 0 to 127
- coarse_inv: float32 [4, 128, 128], P('sub'), as said below
- load: float32 [128, 1024, 384], P(('sub', 'grp')), may hold values from -6 to 6
Outputs:
- solution: float32 [128, 1024, 384], P(('sub', 'grp'))
Inputs may be any that keep to these rules, and one draw needn't show every extreme that they name: `partner`: within the 4 subdomains of one device, the entries form a permutation of 0 to 15. `schur`: each matrix is symmetric positive definite. `coarse_inv`: each matrix is symmetric positive definite.
All inputs are finite; a program needn't handle non-finite values.
Results may differ from a plain program's by a relative error of at most 0.0025.
Values may be sent and summed in bfloat16 or wider, within the bound.
No kernel may reach another device: no remote copies, remote signals or barrier semaphores. Data moves between devices by JAX's collectives and lax.ppermute only.
A program may use at most 128 MiB of HBM per device.

v0:
```python
import jax
import jax.numpy as jnp
from jax import lax
from jax.sharding import PartitionSpec as P

ITERS = 2


def shifted(block, axis, distance):
    devices = range(lax.axis_size(axis))
    route = [((i - distance) % len(devices), i) for i in devices]
    return lax.ppermute(block, axis, route)


def face_terms(direction, schur, mortar, partner):
    subdoms = direction.shape[0]
    order = direction.shape[1]
    columns = direction.shape[2]
    faces_all = mortar.shape[1]
    block = mortar.shape[2]
    half_faces = faces_all // 2
    dir_half = direction.astype(jnp.bfloat16)
    stiff = jnp.einsum("sij,sjr->sir", schur, dir_half, preferred_element_type=jnp.float32)
    face_rows = dir_half.reshape(subdoms, faces_all, block, columns)
    traces = jnp.einsum(
        "sfij,sfjr->sfir", mortar, face_rows, preferred_element_type=jnp.float32
    ).astype(jnp.bfloat16)
    upper = traces[:, :half_faces].reshape(subdoms * half_faces, block, columns)
    lower = traces[:, half_faces:].reshape(subdoms * half_faces, block, columns)
    mates = partner.reshape(-1)
    inverse = jnp.argsort(mates)
    reordered = jnp.take(upper, inverse, axis=0)
    lower_mate = shifted(reordered, "sub", 1)
    jump_lower = (lower.astype(jnp.float32) - lower_mate.astype(jnp.float32)).astype(jnp.bfloat16)
    above = shifted(lower, "sub", -1)
    upper_mate = jnp.take(above, mates, axis=0)
    jump_upper = (upper.astype(jnp.float32) - upper_mate.astype(jnp.float32)).astype(jnp.bfloat16)
    jump_all = jnp.concatenate(
        [
            jump_upper.reshape(subdoms, half_faces, block, columns),
            jump_lower.reshape(subdoms, half_faces, block, columns),
        ],
        axis=1,
    )
    pulled = jnp.einsum("sfji,sfjr->sfir", mortar, jump_all, preferred_element_type=jnp.float32)
    return stiff + pulled.reshape(subdoms, order, columns)


def squares(residual):
    return lax.psum(jnp.sum(residual * residual, axis=(0, 1)), ("sub", "grp"))


def on_device(schur, mortar, partner, corner_map, coarse_inv, load):
    order = load.shape[1]
    corner_count = corner_map.shape[1]
    coarse_count = coarse_inv.shape[1]
    stride = order // corner_count
    onehot = (corner_map[..., None] == jnp.arange(coarse_count, dtype=jnp.int32)).astype(
        jnp.float32
    )
    coarse_matrix = coarse_inv[0]
    solution = jnp.zeros_like(load)
    residual = load
    direction = load
    norm_now = squares(residual)
    for step in range(ITERS):
        partial_value = face_terms(direction, schur, mortar, partner)
        corners = direction[:, ::stride, :]
        local_sum = jnp.einsum("sco,scr->or", onehot, corners, precision=lax.Precision.HIGHEST)
        local_dot = jnp.sum(direction * partial_value, axis=(0, 1))
        coarse_sum = lax.psum(local_sum.astype(jnp.bfloat16), "grp").astype(jnp.float32)
        group_dot = lax.psum(local_dot.astype(jnp.bfloat16), "grp").astype(jnp.float32)
        coarse_val = jnp.dot(coarse_matrix, coarse_sum, precision=lax.Precision.HIGHEST)
        corner_add = jnp.einsum("sco,or->scr", onehot, coarse_val, precision=lax.Precision.HIGHEST)
        image = partial_value.at[:, ::stride, :].add(corner_add)
        curvature = lax.psum(group_dot + jnp.sum(coarse_sum * coarse_val, axis=0), "sub")
        image, curvature = (image, curvature)
        step_len = norm_now / curvature
        solution = solution + step_len * direction
        if step + 1 < ITERS:
            residual = residual - step_len * image
            norm_next = squares(residual)
            direction = residual + norm_next / norm_now * direction
            norm_now = norm_next
    return solution


def solution(mesh):
    return jax.shard_map(
        on_device,
        mesh=mesh,
        in_specs=(
            P(("sub", "grp"), None, None),
            P(("sub", "grp"), None, None, None),
            P(("sub", "grp"), None),
            P(("sub", "grp"), None),
            P("sub", None, None),
            P(("sub", "grp"), None, None),
        ),
        out_specs=P(("sub", "grp"), None, None),
        check_vma=False,
    )
```

profile of v0, /device:TPU:0, one launch (start us, length us, event | category | flops | bytes accessed | tf_op | source)
XLA Modules:
  0.0 398.2 jit_solution(7781319759656753900)
XLA Ops:
  6.5 3.2 convert_element_type.76
  12.3 5.1 %collective-permute-start = (bf16[16,128,384]{2,1,0:T(8,128)(2,1)}, bf16[16,128,384]{2,1,0:T(8,128)(2,1)}, u32[]{:S(2)}, u32[]{:S(2)}) collective-permute-start(bf16[16,128,384]{2,1,0:T(8,128)(2,1)} %bitcast.2), channel_id=1, source_target_pairs={{8,0},{16,8},{24,16},{0,24},{9,1},{17,9},{25,17},{1,25},{10,2},{18... | collective-permute-start | bytes 4718600 | tf_op jit(solution)/shard_map/ppermute | solution.py:12
  20.7 2.8 broadcast_select_fusion.1
  23.5 2.8 slice.20
  27.4 6.6 %copy.8 = f32[4,1024,384]{1,2,0:T(8,128)} copy(f32[4,1024,384]{2,1,0:T(8,128)} %param.13) | data formatting | bytes 12582912 | tf_op args[5]
  34.0 46.9 %all-reduce.3.cloned.1.call-done = bf16[128,384]{1,0:T(8,128)(2,1)} async-done(((bf16[128,384]{1,0:T(8,128)(2,1)}), bf16[128,384]{1,0:T(8,128)(2,1)}) %all-reduce.3.cloned.1.call-update) | async-done | bytes 98320 | tf_op jit(solution)/shard_map/psum | solution.py:71
  82.4 3.3 gather_fusion
  90.4 3.7 fusion.5
  94.1 12.9 %multiply_reduce_fusion.1 = (bf16[384]{0:T(512)(128)(2,1)S(1)}, f32[384]{0:T(512)S(1)}, f32[4,1024,384]{2,1,0:T(8,128)}) fusion(f32[4,1024,384]{2,1,0:T(8,128)S(1)} %bitcast.79, f32[4,8,384,128]{2,3,1,0:T(8,128)} %fusion.5, bf16[4,1024,1024]{2,1,0:T(8,128)(2,1)} %param.8), kind=kOutput, calls=%fused_computation.13 | convolution fusion | flops 3230661632 | bytes 27265280 | tf_op jit(solution)/shard_map/sij,sjr->sir/dot_general | solution.py:23
  107.0 12.8 %psum.57 = bf16[384]{0:T(512)(128)(2,1)S(1)} all-reduce(bf16[384]{0:T(512)(128)(2,1)S(1)} %get-tuple-element.8), channel_id=1, replica_groups=mesh['sub'=4,'grp'=8] {'grp'}, use_global_device_ids=true, to_apply=%region_4.6 | all-reduce | flops 384 | bytes 1536 | tf_op jit(solution)/shard_map/psum | solution.py:72
  119.8 11.7 %psum.59 = f32[384]{0:T(512)S(1)} all-reduce(f32[384]{0:T(512)S(1)} %convert_add_fusion.1), channel_id=1, replica_groups=mesh['sub'=4,'grp'=8] {'sub'}, use_global_device_ids=true, to_apply=%region_7.9 | all-reduce | flops 384 | bytes 3072 | tf_op jit(solution)/shard_map/psum | solution.py:76
  131.5 37.0 %psum.56 = f32[384]{0:T(512)S(1)} all-reduce(f32[384]{0:T(512)S(1)} %get-tuple-element.9), channel_id=1, replica_groups=mesh['sub'=4,'grp'=8] {'sub','grp'}, use_global_device_ids=true, to_apply=%region_1.0 | all-reduce | flops 384 | bytes 3072 | tf_op jit(solution)/shard_map/psum | solution.py:50
  168.5 9.5 %copy.10 = f32[4,1024,384]{2,0,1:T(4,128)} copy(f32[4,1024,384]{2,1,0:T(8,128)} %get-tuple-element.16) | data formatting | bytes 12582912 | tf_op jit(solution)/shard_map/add | solution.py:46
  180.0 7.6 %copy.12 = f32[4,1024,384]{1,2,0:T(8,128)} copy(f32[4,1024,384]{2,0,1:T(4,128)} %scatter_fusion) | data formatting | bytes 12582912 | tf_op jit(solution)/shard_map/scatter-add | solution.py:75
  187.7 5.6 %multiply_reduce_fusion = f32[384]{0:T(512)S(1)} fusion(f32[4,1024,384]{1,2,0:T(8,128)} %copy.8, f32[4,1024,384]{1,2,0:T(8,128)} %copy.12, f32[384]{0:T(512)S(1)} %div.9), kind=kLoop, calls=%fused_computation.11 | loop fusion | flops 6291072 | bytes 12585984 | tf_op jit(solution)/shard_map/reduce_sum | solution.py:50
  193.3 42.2 %psum.60 = f32[384]{0:T(512)S(1)} all-reduce(f32[384]{0:T(512)S(1)} %multiply_reduce_fusion), channel_id=1, replica_groups=mesh['sub'=4,'grp'=8] {'sub','grp'}, use_global_device_ids=true, to_apply=%region_10.12 | all-reduce | flops 384 | bytes 3072 | tf_op jit(solution)/shard_map/psum | solution.py:50
  235.5 7.7 %convert_bitcast_fusion.1 = (bf16[4,48,8,8,128]{4,3,2,1,0:T(8,128)(2,1)S(1)}, f32[4,1024,384]{1,2,0:T(8,128)}) fusion(f32[4,1024,384]{1,2,0:T(8,128)} %copy.8, f32[384]{0:T(512)S(1)} %div.10, f32[4,1024,384]{1,2,0:T(8,128)} %copy.12, f32[384]{0:T(512)S(1)} %div.9), kind=kLoop, calls=%fused_computation.32 | loop fusion | flops 7864320 | bytes 22023168
  249.0 2.8 broadcast_select_fusion
  252.3 4.3 %slice.23 = f32[4,8,384]{1,2,0:T(8,128)S(1)} slice(f32[4,1024,384]{1,2,0:T(8,128)} %get-tuple-element.11), slice={[0:4:1], [0:1024:128], [0:384:1]} | slice | bytes 98304 | tf_op jit(solution)/shard_map/slice | solution.py:68
  257.9 53.1 %all-reduce.5.cloned.1.call-done = bf16[128,384]{1,0:T(8,128)(2,1)} async-done(((bf16[128,384]{1,0:T(8,128)(2,1)}), bf16[128,384]{1,0:T(8,128)(2,1)}) %all-reduce.5.cloned.1.call-update) | async-done | bytes 98320 | tf_op jit(solution)/shard_map/psum | solution.py:71
  312.1 2.8 collective-permute-done.2
  314.9 3.3 gather_fusion.2
  318.3 3.2 subtract_convert_fusion.1
  323.3 3.4 subtract_convert_fusion
  326.8 2.6 copy.17
  329.3 5.1 %fusion.9 = f32[4,8,384,128]{2,3,1,0:T(8,128)} fusion(bf16[4,8,128,128]{3,2,1,0:T(8,128)(2,1)S(1)} %copy-done, bf16[4,4,128,384]{3,2,1,0:T(8,128)(2,1)} %bitcast.87, bf16[4,4,128,384]{3,2,1,0:T(8,128)(2,1)S(1)} %bitcast.85), kind=kOutput, calls=%fused_computation.22 | convolution fusion | flops 404226048 | bytes 10485760 | tf_op jit(solution)/shard_map/sfji,sfjr->sfir/dot_general | solution.py:45
  334.4 6.5 %copy.27 = f32[4,1024,384]{1,2,0:T(8,128)} copy(f32[4,1024,384]{2,1,0:T(8,128)} %bitcast.80) | data formatting | bytes 12582912 | tf_op jit(solution)/shard_map/reshape | solution.py:46
  340.9 12.5 %fusion.1 = bf16[384]{0:T(512)(128)(2,1)S(1)} fusion(f32[4,1024,384]{1,2,0:T(8,128)} %get-tuple-element.11, f32[4,1024,384]{1,2,0:T(8,128)} %copy.27, bf16[4,1024,1024]{2,1,0:T(8,128)(2,1)} %param.8), kind=kOutput, calls=%fused_computation.8 | convolution fusion | flops 3227516416 | bytes 20972288 | tf_op jit(solution)/shard_map/sij,sjr->sir/dot_general | solution.py:23
  353.5 11.8 %psum.61 = bf16[384]{0:T(512)(128)(2,1)S(1)} all-reduce(bf16[384]{0:T(512)(128)(2,1)S(1)} %fusion.1), channel_id=1, replica_groups=mesh['sub'=4,'grp'=8] {'grp'}, use_global_device_ids=true, to_apply=%region_12.14 | all-reduce | flops 384 | bytes 1536 | tf_op jit(solution)/shard_map/psum | solution.py:72
  365.3 9.9 %psum.63 = f32[384]{0:T(512)S(1)} all-reduce(f32[384]{0:T(512)S(1)} %convert_add_fusion), channel_id=1, replica_groups=mesh['sub'=4,'grp'=8] {'sub'}, use_global_device_ids=true, to_apply=%region_15.17 | all-reduce | flops 384 | bytes 3072 | tf_op jit(solution)/shard_map/psum | solution.py:76
  375.2 9.6 %multiply_add_fusion = f32[4,1024,384]{1,2,0:T(8,128)} fusion(f32[4,1024,384]{1,2,0:T(8,128)} %get-tuple-element.11, f32[4,1024,384]{1,2,0:T(8,128)} %copy.8, f32[384]{0:T(512)S(1)} %div.11, f32[384]{0:T(512)S(1)} %div.9), kind=kLoop, calls=%fused_computation.9 | loop fusion | flops 4718592 | bytes 18877440 | tf_op jit(solution)/shard_map/add | solution.py:79
  384.8 6.6 %copy.21 = f32[4,1024,384]{2,1,0:T(8,128)} copy(f32[4,1024,384]{1,2,0:T(8,128)} %multiply_add_fusion) | data formatting | bytes 12582912 | tf_op jit(solution)/shard_map/add | solution.py:79
  (54 shorter events, 25.8 us)
Async XLA Ops:
  6.5 3.2 copy-start
  6.5 74.4 %all-reduce.3.cloned.1.call-start = ((), (), s32[]{:S(2)}) async-start(), calls=%async_computation | async-start | bytes 196608 | tf_op jit(solution)/shard_map/psum | solution.py:71
  10.8 6.6 %copy-start.3 = (s32[4,4]{1,0:T(4,128)S(1)}, s32[4,4]{1,0:T(4,128)}, u32[]{:S(2)}) copy-start(s32[4,4]{1,0:T(4,128)} %param.10) | copy-start | bytes 196
  12.3 70.1 %collective-permute-start = (bf16[16,128,384]{2,1,0:T(8,128)(2,1)}, bf16[16,128,384]{2,1,0:T(8,128)(2,1)}, u32[]{:S(2)}, u32[]{:S(2)}) collective-permute-start(bf16[16,128,384]{2,1,0:T(8,128)(2,1)} %bitcast.2), channel_id=1, source_target_pairs={{8,0},{16,8},{24,16},{0,24},{9,1},{17,9},{25,17},{1,25},{10,2},{18... | collective-permute-start | bytes 4718600 | tf_op jit(solution)/shard_map/ppermute | solution.py:12
  18.8 7.5 %copy-start.2 = (s32[4,8]{1,0:T(4,128)S(1)}, s32[4,8]{1,0:T(4,128)}, u32[]{:S(2)}) copy-start(s32[4,8]{1,0:T(4,128)} %param.11) | copy-start | bytes 388
  23.5 64.4 %collective-permute-start.1 = (bf16[16,128,384]{2,1,0:T(8,128)(2,1)}, bf16[16,128,384]{2,1,0:T(8,128)(2,1)}, u32[]{:S(2)}, u32[]{:S(2)}) collective-permute-start(bf16[16,128,384]{2,1,0:T(8,128)(2,1)} %broadcast_select_fusion.1), channel_id=1, source_target_pairs={{24,0},{0,8},{8,16},{16,24},{25,1},{1,9},{9,17},{17,25},{26,2},{2,... | collective-permute-start | bytes 4718600 | tf_op jit(solution)/shard_map/ppermute | solution.py:12
  27.3 283.6 %all-reduce.5.cloned.1.call-start = ((), (), s32[]{:S(2)}) async-start(), calls=%async_computation.1 | async-start | bytes 196608 | tf_op jit(solution)/shard_map/psum | solution.py:71
  27.4 53.5 %copy-start.1 = (f32[1,128,128]{2,1,0:T(8,128)S(1)}, f32[1,128,128]{2,1,0:T(8,128)}, u32[]{:S(2)}) copy-start(f32[1,128,128]{2,1,0:T(8,128)} %param.12) | copy-start | bytes 196612
  87.9 6.2 %slice-start = ((s8[6291456]{0:T(1024)(128)(4,1)}), s8[4194304]{0:T(1024)(128)(4,1)S(1)}, s32[]{:S(2)}) async-start(s8[6291456]{0:T(1024)(128)(4,1)} %bitcast.78), calls=%async_computation.2 | async-start | bytes 8388608
  90.4 3.7 slice-start.1
  245.6 69.3 %collective-permute-start.2 = (bf16[16,128,384]{1,2,0:T(8,128)(2,1)}, bf16[16,128,384]{1,2,0:T(8,128)(2,1)}, u32[]{:S(2)}, u32[]{:S(2)}) collective-permute-start(bf16[16,128,384]{1,2,0:T(8,128)(2,1)} %bitcast.16), channel_id=1, source_target_pairs={{8,0},{16,8},{24,16},{0,24},{9,1},{17,9},{25,17},{1,25},{10,2},{18... | collective-permute-start | bytes 4718600 | tf_op jit(solution)/shard_map/ppermute | solution.py:12
  251.8 71.5 %collective-permute-start.3 = (bf16[16,128,384]{1,2,0:T(8,128)(2,1)}, bf16[16,128,384]{1,2,0:T(8,128)(2,1)}, u32[]{:S(2)}, u32[]{:S(2)}) collective-permute-start(bf16[16,128,384]{1,2,0:T(8,128)(2,1)} %broadcast_select_fusion), channel_id=1, source_target_pairs={{24,0},{0,8},{8,16},{16,24},{25,1},{1,9},{9,17},{17,25},{26,2},{2,... | collective-permute-start | bytes 4718600 | tf_op jit(solution)/shard_map/ppermute | solution.py:12
Sparse Core Ops, SparseCore 0:
  27.4 53.4 all-reduce.2
  258.0 52.8 all-reduce.4
where the time goes:
time: 399 us; the launch traced here: 398 us
  blocking collectives  125 us (31%)
  waiting for transfers between devices  103 us (26%)
  local copies, waits for them, and re-layouts  61.9 us (16%)
  other arithmetic  46.2 us (12%)
  matrix products  41.1 us (10%)
  between operations  13.6 us (3%)
  starting transfers between devices  7.15 us (2%)
    psum x2, waiting for transfers between devices, on_device(): lax.psum(local_sum.astype(jnp.bfloat16), 'grp').astype(jnp.float32)  100 us
    psum x2, blocking collectives, squares(): return lax.psum(jnp.sum(residual * residual, axis=(0, 1)), ('sub', 'grp'))  79.2 us
    dot_general x2, matrix products, face_terms(): jnp.einsum('sij,sjr->sir', schur, dir_half, preferred_element_type=jnp.fl...  25.4 us
    psum x2, blocking collectives, on_device(): lax.psum(local_dot.astype(jnp.bfloat16), 'grp').astype(jnp.float32)  24.6 us
    psum x2, blocking collectives, on_device(): lax.psum(group_dot + jnp.sum(coarse_sum * coarse_val, axis=0), 'sub')  21.6 us
    add x1, other arithmetic, on_device(): solution = solution + step_len * direction  9.61 us
    add x1, local copies, waits for them, and re-layouts, face_terms(): return stiff + pulled.reshape(subdoms, order, columns)  9.48 us
    dot_general x2, matrix products, face_terms(): jnp.einsum('sfji,sfjr->sfir', mortar, jump_all, preferred_element_type=jn...  8.78 us
  transfers between devices with their start and end apart: 6, of which 3 were waited for; matrix products, arithmetic and copies ran while one was open for 11% of the time, Pallas kernels for 0%

commit v1 on v0

--- a/solution.py
+++ b/solution.py
@@ -4,6 +4,12 @@
 from jax.sharding import PartitionSpec as P
 
 ITERS = 2
+
+
+def cover_weights(z, a_name, named_axis):
+    for nth in (a_name, named_axis):
+        z = lax.psum(z, nth)
+    return z
 
 
 def shifted(block, axis, distance):
@@ -47,7 +53,7 @@
 
 
 def squares(residual):
-    return lax.psum(jnp.sum(residual * residual, axis=(0, 1)), ("sub", "grp"))
+    return cover_weights(jnp.sum(residual * residual, axis=(0, 1)), "grp", "sub")
 
 
 def on_device(schur, mortar, partner, corner_map, coarse_inv, load):

time: 399 us -> 352 us (0.88)
  blocking collectives: 125 us -> 81 us
    psum x2 -> x4, blocking collectives: 79.2 us -> 43.8 us  [cover_weights(): z = lax.psum(z, nth)]
    psum x2 -> x1, blocking collectives: 21.6 us -> 11.7 us  [on_device(): lax.psum(group_dot + jnp.sum(coarse_sum * coarse_val, axis=0), 'sub')]
  transfers between devices with their start and end apart: 6 -> 6, of which waited for: 3 -> 2; matrix products, arithmetic and copies ran while one was open for 11% -> 12% of each run, Pallas kernels for 0% -> 0%
where the time goes in v1:
time: 352 us; the launch traced here: 351 us
  waiting for transfers between devices  99.6 us (28%)
  blocking collectives  81 us (23%)
  local copies, waits for them, and re-layouts  61.9 us (18%)
  other arithmetic  46.2 us (13%)
  matrix products  41.1 us (12%)
  between operations  13.6 us (4%)
  starting transfers between devices  7.15 us (2%)
    psum x2, waiting for transfers between devices, on_device(): lax.psum(local_sum.astype(jnp.bfloat16), 'grp').astype(jnp.float32)  99.5 us
    psum x4, blocking collectives, cover_weights(): z = lax.psum(z, nth)  43.8 us
    psum x2, blocking collectives, on_device(): lax.psum(local_dot.astype(jnp.bfloat16), 'grp').astype(jnp.float32)  25.6 us
    dot_general x2, matrix products, face_terms(): jnp.einsum('sij,sjr->sir', schur, dir_half, preferred_element_type=jnp.fl...  25.4 us
    psum x1, blocking collectives, on_device(): lax.psum(group_dot + jnp.sum(coarse_sum * coarse_val, axis=0), 'sub')  11.7 us
    add x1, other arithmetic, on_device(): solution = solution + step_len * direction  9.61 us
    add x1, local copies, waits for them, and re-layouts, face_terms(): return stiff + pulled.reshape(subdoms, order, columns)  9.48 us
    dot_general x2, matrix products, face_terms(): jnp.einsum('sfji,sfjr->sfir', mortar, jump_all, preferred_element_type=jn...  8.78 us
  transfers between devices with their start and end apart: 6, of which 2 were waited for; matrix products, arithmetic and copies ran while one was open for 12% of the time, Pallas kernels for 0%

profile of v1, /device:TPU:0, one launch (start us, length us, event | category | flops | bytes accessed | tf_op | source)
XLA Modules:
  0.0 350.6 jit_solution(14547406304257943895)
XLA Ops:
  6.5 3.2 convert_element_type.76
  12.3 5.1 %collective-permute-start = (bf16[16,128,384]{2,1,0:T(8,128)(2,1)}, bf16[16,128,384]{2,1,0:T(8,128)(2,1)}, u32[]{:S(2)}, u32[]{:S(2)}) collective-permute-start(bf16[16,128,384]{2,1,0:T(8,128)(2,1)} %bitcast.2), channel_id=1, source_target_pairs={{8,0},{16,8},{24,16},{0,24},{9,1},{17,9},{25,17},{1,25},{10,2},{18... | collective-permute-start | bytes 4718600 | tf_op jit(solution)/shard_map/ppermute | solution.py:18
  20.7 2.8 broadcast_select_fusion.1
  23.5 2.8 slice.20
  27.4 6.6 %copy.8 = f32[4,1024,384]{1,2,0:T(8,128)} copy(f32[4,1024,384]{2,1,0:T(8,128)} %param.13) | data formatting | bytes 12582912 | tf_op args[5]
  34.0 46.9 %all-reduce.4.cloned.1.call-done = bf16[128,384]{1,0:T(8,128)(2,1)} async-done(((bf16[128,384]{1,0:T(8,128)(2,1)}), bf16[128,384]{1,0:T(8,128)(2,1)}) %all-reduce.4.cloned.1.call-update) | async-done | bytes 98320 | tf_op jit(solution)/shard_map/psum | solution.py:77
  82.4 3.3 gather_fusion
  90.4 3.7 %fusion.5 = f32[4,8,384,128]{2,3,1,0:T(8,128)} fusion(bf16[4,8,128,128]{3,2,1,0:T(8,128)(2,1)S(1)} %copy-done, bf16[4,4,128,384]{3,2,1,0:T(8,128)(2,1)S(1)} %bitcast.86, bf16[4,4,128,384]{3,2,1,0:T(8,128)(2,1)S(1)} %bitcast.84), kind=kOutput, calls=%fused_computation.18 | convolution fusion | flops 404226048 | bytes 10485760 | tf_op jit(solution)/shard_map/sfji,sfjr->sfir/dot_general | solution.py:51
  94.1 12.9 %multiply_reduce_fusion.1 = (bf16[384]{0:T(512)(128)(2,1)S(1)}, f32[384]{0:T(512)S(1)}, f32[4,1024,384]{2,1,0:T(8,128)}) fusion(f32[4,1024,384]{2,1,0:T(8,128)S(1)} %bitcast.79, f32[4,8,384,128]{2,3,1,0:T(8,128)} %fusion.5, bf16[4,1024,1024]{2,1,0:T(8,128)(2,1)} %param.8), kind=kOutput, calls=%fused_computation.13 | convolution fusion | flops 3230661632 | bytes 27265280 | tf_op jit(solution)/shard_map/sij,sjr->sir/dot_general | solution.py:29
  107.0 12.8 %psum.72 = bf16[384]{0:T(512)(128)(2,1)S(1)} all-reduce(bf16[384]{0:T(512)(128)(2,1)S(1)} %get-tuple-element.8), channel_id=1, replica_groups=mesh['sub'=4,'grp'=8] {'grp'}, use_global_device_ids=true, to_apply=%region_5.7 | all-reduce | flops 384 | bytes 1536 | tf_op jit(solution)/shard_map/psum | solution.py:78
  119.8 12.0 %psum.70 = f32[384]{0:T(512)S(1)} all-reduce(f32[384]{0:T(512)S(1)} %get-tuple-element.9), channel_id=1, replica_groups=mesh['sub'=4,'grp'=8] {'grp'}, use_global_device_ids=true, to_apply=%region_1.0 | all-reduce | flops 384 | bytes 3072 | tf_op jit(solution)/shard_map/psum | solution.py:11
  131.8 9.5 %copy.10 = f32[4,1024,384]{2,0,1:T(4,128)} copy(f32[4,1024,384]{2,1,0:T(8,128)} %get-tuple-element.18) | data formatting | bytes 12582912 | tf_op jit(solution)/shard_map/add | solution.py:52
  143.3 7.6 %copy.12 = f32[4,1024,384]{1,2,0:T(8,128)} copy(f32[4,1024,384]{2,0,1:T(4,128)} %scatter_fusion) | data formatting | bytes 12582912 | tf_op jit(solution)/shard_map/scatter-add | solution.py:81
  151.0 11.7 %all-reduce = (f32[384]{0:T(512)S(1)}, f32[384]{0:T(512)S(1)}) all-reduce(f32[384]{0:T(512)S(1)} %psum.70, f32[384]{0:T(512)S(1)} %convert_add_fusion.1), channel_id=1, replica_groups=mesh['sub'=4,'grp'=8] {'sub'}, use_global_device_ids=true, to_apply=%region_2.0 | all-reduce | flops 768 | bytes 6144 | tf_op jit(solution)/shard_map/psum | solution.py:11
  162.6 5.6 %multiply_reduce_fusion = f32[384]{0:T(512)S(1)} fusion(f32[4,1024,384]{1,2,0:T(8,128)} %copy.8, f32[4,1024,384]{1,2,0:T(8,128)} %copy.12, f32[384]{0:T(512)S(1)} %div.9), kind=kLoop, calls=%fused_computation.11 | loop fusion | flops 6291072 | bytes 12585984 | tf_op jit(solution)/shard_map/reduce_sum | solution.py:56
  168.2 11.8 %psum.75 = f32[384]{0:T(512)S(1)} all-reduce(f32[384]{0:T(512)S(1)} %multiply_reduce_fusion), channel_id=1, replica_groups=mesh['sub'=4,'grp'=8] {'grp'}, use_global_device_ids=true, to_apply=%region_11.13 | all-reduce | flops 384 | bytes 3072 | tf_op jit(solution)/shard_map/psum | solution.py:11
  180.0 8.4 %psum.76 = f32[384]{0:T(512)S(1)} all-reduce(f32[384]{0:T(512)S(1)} %psum.75), channel_id=1, replica_groups=mesh['sub'=4,'grp'=8] {'sub'}, use_global_device_ids=true, to_apply=%region_12.14 | all-reduce | flops 384 | bytes 3072 | tf_op jit(solution)/shard_map/psum | solution.py:11
  188.4 7.7 %convert_bitcast_fusion.1 = (bf16[4,48,8,8,128]{4,3,2,1,0:T(8,128)(2,1)S(1)}, f32[4,1024,384]{1,2,0:T(8,128)}) fusion(f32[4,1024,384]{1,2,0:T(8,128)} %copy.8, f32[384]{0:T(512)S(1)} %div.10, f32[4,1024,384]{1,2,0:T(8,128)} %copy.12, f32[384]{0:T(512)S(1)} %div.9), kind=kLoop, calls=%fused_computation.32 | loop fusion | flops 7864320 | bytes 22023168
  202.4 2.8 broadcast_select_fusion
  205.2 4.3 %slice.23 = f32[4,8,384]{1,2,0:T(8,128)S(1)} slice(f32[4,1024,384]{1,2,0:T(8,128)} %get-tuple-element.13), slice={[0:4:1], [0:1024:128], [0:384:1]} | slice | bytes 98304 | tf_op jit(solution)/shard_map/slice | solution.py:74
  210.8 52.6 %all-reduce.6.cloned.1.call-done = bf16[128,384]{1,0:T(8,128)(2,1)} async-done(((bf16[128,384]{1,0:T(8,128)(2,1)}), bf16[128,384]{1,0:T(8,128)(2,1)}) %all-reduce.6.cloned.1.call-update) | async-done | bytes 98320 | tf_op jit(solution)/shard_map/psum | solution.py:77
  264.6 3.3 gather_fusion.2
  267.9 3.2 subtract_convert_fusion.1
  273.0 3.4 subtract_convert_fusion
  276.4 2.6 copy.17
  279.0 5.1 %fusion.9 = f32[4,8,384,128]{2,3,1,0:T(8,128)} fusion(bf16[4,8,128,128]{3,2,1,0:T(8,128)(2,1)S(1)} %copy-done, bf16[4,4,128,384]{3,2,1,0:T(8,128)(2,1)} %bitcast.87, bf16[4,4,128,384]{3,2,1,0:T(8,128)(2,1)S(1)} %bitcast.85), kind=kOutput, calls=%fused_computation.22 | convolution fusion | flops 404226048 | bytes 10485760 | tf_op jit(solution)/shard_map/sfji,sfjr->sfir/dot_general | solution.py:51
  284.1 6.5 %copy.27 = f32[4,1024,384]{1,2,0:T(8,128)} copy(f32[4,1024,384]{2,1,0:T(8,128)} %bitcast.80) | data formatting | bytes 12582912 | tf_op jit(solution)/shard_map/reshape | solution.py:52
  290.6 12.5 %fusion.1 = bf16[384]{0:T(512)(128)(2,1)S(1)} fusion(f32[4,1024,384]{1,2,0:T(8,128)} %get-tuple-element.13, f32[4,1024,384]{1,2,0:T(8,128)} %copy.27, bf16[4,1024,1024]{2,1,0:T(8,128)(2,1)} %param.8), kind=kOutput, calls=%fused_computation.8 | convolution fusion | flops 3227516416 | bytes 20972288 | tf_op jit(solution)/shard_map/sij,sjr->sir/dot_general | solution.py:29
  303.1 12.8 %psum.77 = bf16[384]{0:T(512)(128)(2,1)S(1)} all-reduce(bf16[384]{0:T(512)(128)(2,1)S(1)} %fusion.1), channel_id=1, replica_groups=mesh['sub'=4,'grp'=8] {'grp'}, use_global_device_ids=true, to_apply=%region_14.16 | all-reduce | flops 384 | bytes 1536 | tf_op jit(solution)/shard_map/psum | solution.py:78
  315.9 11.7 %psum.79 = f32[384]{0:T(512)S(1)} all-reduce(f32[384]{0:T(512)S(1)} %convert_add_fusion), channel_id=1, replica_groups=mesh['sub'=4,'grp'=8] {'sub'}, use_global_device_ids=true, to_apply=%region_17.19 | all-reduce | flops 384 | bytes 3072 | tf_op jit(solution)/shard_map/psum | solution.py:82
  327.6 9.6 %multiply_add_fusion = f32[4,1024,384]{1,2,0:T(8,128)} fusion(f32[4,1024,384]{1,2,0:T(8,128)} %get-tuple-element.13, f32[4,1024,384]{1,2,0:T(8,128)} %copy.8, f32[384]{0:T(512)S(1)} %div.11, f32[384]{0:T(512)S(1)} %div.9), kind=kLoop, calls=%fused_computation.9 | loop fusion | flops 4718592 | bytes 18877440 | tf_op jit(solution)/shard_map/add | solution.py:85
  337.2 6.6 %copy.21 = f32[4,1024,384]{2,1,0:T(8,128)} copy(f32[4,1024,384]{1,2,0:T(8,128)} %multiply_add_fusion) | data formatting | bytes 12582912 | tf_op jit(solution)/shard_map/add | solution.py:85
  (55 shorter events, 25.8 us)
Async XLA Ops:
  6.5 3.2 copy-start
  6.5 74.4 %all-reduce.4.cloned.1.call-start = ((), (), s32[]{:S(2)}) async-start(), calls=%async_computation | async-start | bytes 196608 | tf_op jit(solution)/shard_map/psum | solution.py:77
  10.8 6.6 %copy-start.3 = (s32[4,4]{1,0:T(4,128)S(1)}, s32[4,4]{1,0:T(4,128)}, u32[]{:S(2)}) copy-start(s32[4,4]{1,0:T(4,128)} %param.10) | copy-start | bytes 196
  12.3 70.1 %collective-permute-start = (bf16[16,128,384]{2,1,0:T(8,128)(2,1)}, bf16[16,128,384]{2,1,0:T(8,128)(2,1)}, u32[]{:S(2)}, u32[]{:S(2)}) collective-permute-start(bf16[16,128,384]{2,1,0:T(8,128)(2,1)} %bitcast.2), channel_id=1, source_target_pairs={{8,0},{16,8},{24,16},{0,24},{9,1},{17,9},{25,17},{1,25},{10,2},{18... | collective-permute-start | bytes 4718600 | tf_op jit(solution)/shard_map/ppermute | solution.py:18
  18.8 7.5 %copy-start.2 = (s32[4,8]{1,0:T(4,128)S(1)}, s32[4,8]{1,0:T(4,128)}, u32[]{:S(2)}) copy-start(s32[4,8]{1,0:T(4,128)} %param.11) | copy-start | bytes 388
  23.5 64.4 %collective-permute-start.1 = (bf16[16,128,384]{2,1,0:T(8,128)(2,1)}, bf16[16,128,384]{2,1,0:T(8,128)(2,1)}, u32[]{:S(2)}, u32[]{:S(2)}) collective-permute-start(bf16[16,128,384]{2,1,0:T(8,128)(2,1)} %broadcast_select_fusion.1), channel_id=1, source_target_pairs={{24,0},{0,8},{8,16},{16,24},{25,1},{1,9},{9,17},{17,25},{26,2},{2,... | collective-permute-start | bytes 4718600 | tf_op jit(solution)/shard_map/ppermute | solution.py:18
  27.3 236.1 %all-reduce.6.cloned.1.call-start = ((), (), s32[]{:S(2)}) async-start(), calls=%async_computation.1 | async-start | bytes 196608 | tf_op jit(solution)/shard_map/psum | solution.py:77
  27.4 53.5 %copy-start.1 = (f32[1,128,128]{2,1,0:T(8,128)S(1)}, f32[1,128,128]{2,1,0:T(8,128)}, u32[]{:S(2)}) copy-start(f32[1,128,128]{2,1,0:T(8,128)} %param.12) | copy-start | bytes 196612
  87.9 6.2 %slice-start = ((s8[6291456]{0:T(1024)(128)(4,1)}), s8[4194304]{0:T(1024)(128)(4,1)S(1)}, s32[]{:S(2)}) async-start(s8[6291456]{0:T(1024)(128)(4,1)} %bitcast.78), calls=%async_computation.2 | async-start | bytes 8388608
  90.4 3.7 %slice-start.1 = ((s8[6291456]{0:T(1024)(128)(4,1)}), s8[2097152]{0:T(1024)(128)(4,1)S(1)}, s32[]{:S(2)}) async-start(s8[6291456]{0:T(1024)(128)(4,1)} %bitcast.78), calls=%async_computation.3 | async-start | bytes 4194304
  198.5 66.1 %collective-permute-start.2 = (bf16[16,128,384]{1,2,0:T(8,128)(2,1)}, bf16[16,128,384]{1,2,0:T(8,128)(2,1)}, u32[]{:S(2)}, u32[]{:S(2)}) collective-permute-start(bf16[16,128,384]{1,2,0:T(8,128)(2,1)} %bitcast.16), channel_id=1, source_target_pairs={{8,0},{16,8},{24,16},{0,24},{9,1},{17,9},{25,17},{1,25},{10,2},{18... | collective-permute-start | bytes 4718600 | tf_op jit(solution)/shard_map/ppermute | solution.py:18
  205.2 67.8 %collective-permute-start.3 = (bf16[16,128,384]{1,2,0:T(8,128)(2,1)}, bf16[16,128,384]{1,2,0:T(8,128)(2,1)}, u32[]{:S(2)}, u32[]{:S(2)}) collective-permute-start(bf16[16,128,384]{1,2,0:T(8,128)(2,1)} %broadcast_select_fusion), channel_id=1, source_target_pairs={{24,0},{0,8},{8,16},{16,24},{25,1},{1,9},{9,17},{17,25},{26,2},{2,... | collective-permute-start | bytes 4718600 | tf_op jit(solution)/shard_map/ppermute | solution.py:18
Sparse Core Ops, SparseCore 0:
  27.4 53.4 all-reduce.3
  210.9 52.4 all-reduce.5
